TPU v7x, 32 devices: a whole 2x2x4 slice. The times are simulated.
32 devices in a mesh: src: 8 (over z, x), tgt: 4 (over y, core).
Axes of the slice: x: 2, y: 2, z: 4, core: 2. Of those that a mesh axis runs over, the one named last changes fastest.
Arguments:
- source_words: bfloat16 [4096, 300], P(('src', 'tgt')), may hold values from -3 to 3
- target_words: bfloat16 [3840, 300], P(('tgt', 'src')), may hold values from -24 to 24
Outputs:
- rotated: bfloat16 [4096, 300], P(('src', 'tgt'))
- matched: float32 [4096, 300], P(('src', 'tgt'))
- ortho: float32 [300, 300], replicated
- row_pot: float32 [4096], P(('src', 'tgt'))
- col_pot: float32 [3840], P(('tgt', 'src'))
All inputs are finite; a program needn't handle non-finite values.
Results may differ from a plain program's by a relative error of at most 0.0034.
Values may be sent and summed in bfloat16 or wider, within the bound.
No kernel may reach another device: no remote copies, remote signals or barrier semaphores. Data moves between devices by JAX's collectives and lax.ppermute only.
A program may use at most 64 MiB of HBM per device.

v0:
```python
import math
import jax
import jax.numpy as jnp
from jax import lax
from jax.sharding import PartitionSpec as P

ITERS = 2
NEWTON = 12


def reduce_rows(top, total):
    higher = lax.pmax(top, "tgt")
    whole = lax.psum(total * jnp.exp(top - higher), "tgt")
    return -(higher + jnp.log(whole))


def reduce_cols(top, total):
    higher = lax.pmax(top, "src")
    whole = lax.psum(total * jnp.exp(top - higher), "src")
    return -(higher + jnp.log(whole))


def body(source_words, target_words):
    width = source_words.shape[1]
    scale = 4.0 / math.sqrt(width)
    highest = lax.Precision.HIGHEST
    src_block = lax.all_gather(source_words, "tgt", axis=0, tiled=True)
    rows = src_block.shape[0]
    cols = target_words.shape[0] * lax.axis_size("src")
    inner = (((1,), (1,)), ((), ()))
    leading = (((0,), (0,)), ((), ()))

    def scores(piece):
        return lax.dot_general(src_block, piece, inner, preferred_element_type=jnp.float32) * scale

    col_pot = jnp.zeros((cols,), jnp.float32)
    row_pot = jnp.zeros((rows,), jnp.float32)
    for sweep_index in range(ITERS):
        row_top = jnp.full((rows,), -jnp.inf, jnp.float32)
        total = jnp.zeros((rows,), jnp.float32)
        row_shift = col_pot
        row_logits = (
            scores(lax.all_gather(target_words, "src", axis=0, tiled=True)) + row_shift[None, :]
        )
        higher = jnp.max(row_logits, axis=1)
        total = total * jnp.exp(row_top - higher) + jnp.sum(
            jnp.exp(row_logits - higher[:, None]), axis=1
        )
        top, total = (higher, total)
        row_pot = reduce_rows(top, total)
        logits = scores(lax.all_gather(target_words, "src", axis=0, tiled=True)) + row_pot[:, None]
        col_top = jnp.max(logits, axis=0)
        parts = jnp.stack([col_top, jnp.sum(jnp.exp(logits - col_top[None, :]), axis=0)])
        col_pot = reduce_cols(parts[0], parts[1])
    piece = lax.all_gather(target_words, "src", axis=0, tiled=True)
    plan = jnp.exp(scores(piece) + row_pot[:, None] + col_pot[None, :]).astype(jnp.bfloat16)
    summed = jnp.dot(plan, piece, preferred_element_type=jnp.float32)
    matched = lax.psum_scatter(summed, "tgt", scatter_dimension=0, tiled=True)
    term = lax.dot_general(source_words.astype(jnp.float32), matched, leading, precision=highest)
    cov = lax.psum(term, ("src", "tgt"))
    ortho = cov / jnp.sqrt(jnp.sum(cov * cov) + 1e-06)
    for step_index in range(NEWTON):
        ortho = 1.5 * ortho - 0.5 * jnp.dot(
            ortho, jnp.dot(ortho.T, ortho, precision=highest), precision=highest
        )
    rotated = jnp.dot(source_words.astype(jnp.float32), ortho, precision=highest).astype(
        jnp.bfloat16
    )
    own_rows = rows // lax.axis_size("tgt")
    own_cols = cols // lax.axis_size("src")
    row_part = lax.dynamic_slice_in_dim(row_pot, lax.axis_index("tgt") * own_rows, own_rows)
    col_part = lax.dynamic_slice_in_dim(col_pot, lax.axis_index("src") * own_cols, own_cols)
    return (rotated, matched, ortho, row_part, col_part)


def solution(mesh):
    in_specs = (P(("src", "tgt"), None), P(("tgt", "src"), None))
    out_specs = (
        P(("src", "tgt"), None),
        P(("src", "tgt"), None),
        P(),
        P(("src", "tgt")),
        P(("tgt", "src")),
    )
    return jax.shard_map(body, mesh=mesh, in_specs=in_specs, out_specs=out_specs, check_vma=False)
```

profile of v0, /device:TPU:0, one launch (start us, length us, event | category | flops | bytes accessed | tf_op | source)
XLA Modules:
  0.0 346.5 jit_solution(8478248790256403142)
XLA Ops:
  7.2 33.5 %all-gather = bf16[8,120,300]{1,2,0:T(8,128)(2,1)S(1)} all-gather(bf16[1,120,300]{1,2,0:T(8,128)(2,1)} %bitcast.59), channel_id=1, replica_groups=mesh['src'=8,'tgt'=4] {'src'}, dimensions={0}, use_global_device_ids=true | all-gather | bytes 648000 | tf_op jit(solution)/shard_map/all_gather | solution.py:55
  41.4 6.1 %all_gather.4 = bf16[512,300]{0,1:T(8,128)(2,1)S(1)} all-gather(bf16[128,300]{0,1:T(8,128)(2,1)S(1)} %copy-done), channel_id=1, replica_groups=mesh['src'=8,'tgt'=4] {'tgt'}, dimensions={0}, use_global_device_ids=true | all-gather | bytes 384000 | tf_op jit(solution)/shard_map/all_gather | solution.py:27
  48.3 7.0 %pmax.28 = f32[512]{0:T(512)S(1)} all-reduce(f32[512]{0:T(512)S(1)} %get-tuple-element.20), channel_id=1, replica_groups=mesh['src'=8,'tgt'=4] {'tgt'}, use_global_device_ids=true, to_apply=%region_1.0 | all-reduce | flops 512 | bytes 4096 | tf_op jit(solution)/shard_map/pmax | solution.py:12
  55.6 5.7 %psum.35 = f32[512]{0:T(512)S(1)} all-reduce(f32[512]{0:T(512)S(1)} %exponential_multiply_fusion.3), channel_id=1, replica_groups=mesh['src'=8,'tgt'=4] {'tgt'}, use_global_device_ids=true, to_apply=%region_3.0 | all-reduce | flops 512 | bytes 4096 | tf_op jit(solution)/shard_map/psum | solution.py:13
  62.0 21.5 %pmax.29 = f32[960]{0:T(1024)S(1)} all-reduce(f32[960]{0:T(1024)S(1)} %add_reduce_fusion.1), channel_id=1, replica_groups=mesh['src'=8,'tgt'=4] {'src'}, use_global_device_ids=true, to_apply=%region_5.0 | all-reduce | flops 960 | bytes 7680 | tf_op jit(solution)/shard_map/pmax | solution.py:18
  83.5 17.1 %psum.36 = f32[960]{0:T(1024)S(1)} all-reduce(f32[960]{0:T(1024)S(1)} %exponential_multiply_fusion.1), channel_id=1, replica_groups=mesh['src'=8,'tgt'=4] {'src'}, use_global_device_ids=true, to_apply=%region_7.0 | all-reduce | flops 960 | bytes 7680 | tf_op jit(solution)/shard_map/psum | solution.py:19
  101.3 5.7 %pmax.30 = f32[512]{0:T(512)S(1)} all-reduce(f32[512]{0:T(512)S(1)} %add_reduce_fusion), channel_id=1, replica_groups=mesh['src'=8,'tgt'=4] {'tgt'}, use_global_device_ids=true, to_apply=%region_9.0 | all-reduce | flops 512 | bytes 4096 | tf_op jit(solution)/shard_map/pmax | solution.py:12
  107.0 6.0 %psum.37 = f32[512]{0:T(512)S(1)} all-reduce(f32[512]{0:T(512)S(1)} %exponential_multiply_fusion.2), channel_id=1, replica_groups=mesh['src'=8,'tgt'=4] {'tgt'}, use_global_device_ids=true, to_apply=%region_11.0 | all-reduce | flops 512 | bytes 4096 | tf_op jit(solution)/shard_map/psum | solution.py:13
  113.8 19.1 %pmax.31 = f32[960]{0:T(1024)S(1)} all-reduce(f32[960]{0:T(1024)S(1)} %add_reduce_fusion.2), channel_id=1, replica_groups=mesh['src'=8,'tgt'=4] {'src'}, use_global_device_ids=true, to_apply=%region_13.0 | all-reduce | flops 960 | bytes 7680 | tf_op jit(solution)/shard_map/pmax | solution.py:18
  133.0 17.2 %psum.38 = f32[960]{0:T(1024)S(1)} all-reduce(f32[960]{0:T(1024)S(1)} %exponential_multiply_fusion), channel_id=1, replica_groups=mesh['src'=8,'tgt'=4] {'src'}, use_global_device_ids=true, to_apply=%region_15.0 | all-reduce | flops 960 | bytes 7680 | tf_op jit(solution)/shard_map/psum | solution.py:19
  150.2 1.4 fusion.13
  151.9 20.7 %reduce-scatter.2.cloned.1.call-done = f32[128,300]{0,1:T(8,128)} async-done(((f32[512,300]{0,1:T(8,128)}), f32[128,300]{0,1:T(8,128)}) %reduce-scatter.2.cloned.1.call-update) | async-done | bytes 153616 | tf_op jit(solution)/shard_map/reduce_scatter | solution.py:58
  172.5 2.0 convolution_bitcast_fusion
  175.7 130.6 %all-reduce.2.cloned.1.call-done = f32[300,300]{0,1:T(8,128)} async-done(((f32[300,300]{0,1:T(8,128)}), f32[300,300]{0,1:T(8,128)}) %all-reduce.2.cloned.1.call-update) | async-done | bytes 360016 | tf_op jit(solution)/shard_map/psum | solution.py:60
  306.3 1.8 multiply_reduce_fusion
  308.8 2.2 fusion.16
  311.1 1.2 fusion.11
  315.6 1.2 fusion.9
  320.1 1.2 fusion.7
  321.4 1.3 fusion.22
  324.9 1.2 fusion.5
  329.4 1.2 fusion.3
  332.9 1.3 fusion.27
  336.4 1.2 fusion
  (45 shorter events, 23.9 us)
Async XLA Ops:
  7.2 34.2 %copy-start = (bf16[128,300]{0,1:T(8,128)(2,1)S(1)}, bf16[128,300]{0,1:T(8,128)(2,1)}, u32[]{:S(2)}) copy-start(bf16[128,300]{0,1:T(8,128)(2,1)} %param.2) | copy-start | bytes 230404
  7.2 165.4 %reduce-scatter.2.cloned.1.call-start = ((), (), s32[]{:S(2)}) async-start(), calls=%async_computation.1 | async-start | bytes 778240 | tf_op jit(solution)/shard_map/reduce_scatter | solution.py:58
  151.6 154.7 %all-reduce.2.cloned.1.call-start = ((), (), s32[]{:S(2)}) async-start(), calls=%async_computation.2 | async-start | bytes 933888 | tf_op jit(solution)/shard_map/psum | solution.py:60
  306.3 4.8 %copy-start.1 = (f32[300,300]{0,1:T(8,128)S(1)}, f32[300,300]{0,1:T(8,128)}, u32[]{:S(2)}) copy-start(f32[300,300]{0,1:T(8,128)} %all-reduce.2.cloned.1.call-done) | copy-start | bytes 1080004
Sparse Core Ops, SparseCore 0:
  151.7 20.7 reduce-scatter.1
  178.4 127.8 all-reduce.1
where the time goes:
time: 347 us; the launch traced here: 346 us
  waiting for transfers between devices  151 us (44%)
  blocking collectives  139 us (40%)
  matrix products  33.8 us (10%)
  between operations  15 us (4%)
  other arithmetic  4.41 us (1%)
    psum x1, waiting for transfers between devices, body(): cov = lax.psum(term, ('src', 'tgt'))  131 us
    pmax x2, blocking collectives, reduce_cols(): higher = lax.pmax(top, 'src')  40.6 us
    psum x2, blocking collectives, reduce_cols(): whole = lax.psum(total * jnp.exp(top - higher), 'src')  34.3 us
    all_gather x1, blocking collectives, body(): piece = lax.all_gather(target_words, 'src', axis=0, tiled=True)  33.5 us
    reduce_scatter x1, waiting for transfers between devices, body(): matched = lax.psum_scatter(summed, 'tgt', scatter_dimension=0, tiled=True)  20.7 us
    dot_general x12, matrix products, body(): jnp.dot(ortho, jnp.dot(ortho.T, ortho, precision=highest), precision=high...  14.5 us
    dot_general x12, matrix products, body(): jnp.dot(ortho.T, ortho, precision=highest)  14.1 us
    pmax x2, blocking collectives, reduce_rows(): higher = lax.pmax(top, 'tgt')  12.6 us
  transfers between devices with their start and end apart: 2, of which 2 were waited for; matrix products, arithmetic and copies ran while one was open for 0% of the time, Pallas kernels for 0%

commit v1 on v0

--- a/solution.py
+++ b/solution.py
@@ -57,7 +57,9 @@
     summed = jnp.dot(plan, piece, preferred_element_type=jnp.float32)
     matched = lax.psum_scatter(summed, "tgt", scatter_dimension=0, tiled=True)
     term = lax.dot_general(source_words.astype(jnp.float32), matched, leading, precision=highest)
-    cov = lax.psum(term, ("src", "tgt"))
+    cov = term
+    for m in ("tgt", "src"):
+        cov = lax.psum(cov, m)
     ortho = cov / jnp.sqrt(jnp.sum(cov * cov) + 1e-06)
     for step_index in range(NEWTON):
         ortho = 1.5 * ortho - 0.5 * jnp.dot(

time: 347 us -> 325 us (0.937)
  waiting for transfers between devices: 151 us -> 129 us
    psum x1 -> x2, waiting for transfers between devices: 131 us -> 109 us  [body(): cov = lax.psum(cov, m)]
  transfers between devices with their start and end apart: 2 -> 3, of which waited for: 2 -> 3; matrix products, arithmetic and copies ran while one was open for 0% -> 0% of each run, Pallas kernels for 0% -> 0%
where the time goes in v1:
time: 325 us; the launch traced here: 324 us
  blocking collectives  139 us (43%)
  waiting for transfers between devices  129 us (40%)
  matrix products  33.8 us (10%)
  between operations  14.7 us (5%)
  other arithmetic  4.41 us (1%)
    psum x2, waiting for transfers between devices, body(): cov = lax.psum(cov, m)  109 us
    pmax x2, blocking collectives, reduce_cols(): higher = lax.pmax(top, 'src')  40.6 us
    psum x2, blocking collectives, reduce_cols(): whole = lax.psum(total * jnp.exp(top - higher), 'src')  34.3 us
    all_gather x1, blocking collectives, body(): piece = lax.all_gather(target_words, 'src', axis=0, tiled=True)  33.5 us
    reduce_scatter x1, waiting for transfers between devices, body(): matched = lax.psum_scatter(summed, 'tgt', scatter_dimension=0, tiled=True)  20.9 us
    dot_general x12, matrix products, body(): jnp.dot(ortho, jnp.dot(ortho.T, ortho, precision=highest), precision=high...  14.8 us
    dot_general x12, matrix products, body(): jnp.dot(ortho.T, ortho, precision=highest)  13.9 us
    pmax x2, blocking collectives, reduce_rows(): higher = lax.pmax(top, 'tgt')  12.6 us
  transfers between devices with their start and end apart: 3, of which 3 were waited for; matrix products, arithmetic and copies ran while one was open for 0% of the time, Pallas kernels for 0%

profile of v1, /device:TPU:0, one launch (start us, length us, event | category | flops | bytes accessed | tf_op | source)
XLA Modules:
  0.0 324.4 jit_solution(1788646350662916822)
XLA Ops:
  7.2 33.5 %all-gather = bf16[8,120,300]{1,2,0:T(8,128)(2,1)S(1)} all-gather(bf16[1,120,300]{1,2,0:T(8,128)(2,1)} %bitcast.59), channel_id=1, replica_groups=mesh['src'=8,'tgt'=4] {'src'}, dimensions={0}, use_global_device_ids=true | all-gather | bytes 648000 | tf_op jit(solution)/shard_map/all_gather | solution.py:55
  41.4 6.1 %all_gather.4 = bf16[512,300]{0,1:T(8,128)(2,1)S(1)} all-gather(bf16[128,300]{0,1:T(8,128)(2,1)S(1)} %copy-done), channel_id=1, replica_groups=mesh['src'=8,'tgt'=4] {'tgt'}, dimensions={0}, use_global_device_ids=true | all-gather | bytes 384000 | tf_op jit(solution)/shard_map/all_gather | solution.py:27
  48.3 7.0 %pmax.28 = f32[512]{0:T(512)S(1)} all-reduce(f32[512]{0:T(512)S(1)} %get-tuple-element.20), channel_id=1, replica_groups=mesh['src'=8,'tgt'=4] {'tgt'}, use_global_device_ids=true, to_apply=%region_1.0 | all-reduce | flops 512 | bytes 4096 | tf_op jit(solution)/shard_map/pmax | solution.py:12
  55.6 5.7 %psum.42 = f32[512]{0:T(512)S(1)} all-reduce(f32[512]{0:T(512)S(1)} %exponential_multiply_fusion.3), channel_id=1, replica_groups=mesh['src'=8,'tgt'=4] {'tgt'}, use_global_device_ids=true, to_apply=%region_3.0 | all-reduce | flops 512 | bytes 4096 | tf_op jit(solution)/shard_map/psum | solution.py:13
  62.0 21.5 %pmax.29 = f32[960]{0:T(1024)S(1)} all-reduce(f32[960]{0:T(1024)S(1)} %add_reduce_fusion.1), channel_id=1, replica_groups=mesh['src'=8,'tgt'=4] {'src'}, use_global_device_ids=true, to_apply=%region_5.0 | all-reduce | flops 960 | bytes 7680 | tf_op jit(solution)/shard_map/pmax | solution.py:18
  83.5 17.1 %psum.43 = f32[960]{0:T(1024)S(1)} all-reduce(f32[960]{0:T(1024)S(1)} %exponential_multiply_fusion.1), channel_id=1, replica_groups=mesh['src'=8,'tgt'=4] {'src'}, use_global_device_ids=true, to_apply=%region_7.0 | all-reduce | flops 960 | bytes 7680 | tf_op jit(solution)/shard_map/psum | solution.py:19
  101.3 5.7 %pmax.30 = f32[512]{0:T(512)S(1)} all-reduce(f32[512]{0:T(512)S(1)} %add_reduce_fusion), channel_id=1, replica_groups=mesh['src'=8,'tgt'=4] {'tgt'}, use_global_device_ids=true, to_apply=%region_9.0 | all-reduce | flops 512 | bytes 4096 | tf_op jit(solution)/shard_map/pmax | solution.py:12
  107.0 6.0 %psum.44 = f32[512]{0:T(512)S(1)} all-reduce(f32[512]{0:T(512)S(1)} %exponential_multiply_fusion.2), channel_id=1, replica_groups=mesh['src'=8,'tgt'=4] {'tgt'}, use_global_device_ids=true, to_apply=%region_11.0 | all-reduce | flops 512 | bytes 4096 | tf_op jit(solution)/shard_map/psum | solution.py:13
  113.8 19.1 %pmax.31 = f32[960]{0:T(1024)S(1)} all-reduce(f32[960]{0:T(1024)S(1)} %add_reduce_fusion.2), channel_id=1, replica_groups=mesh['src'=8,'tgt'=4] {'src'}, use_global_device_ids=true, to_apply=%region_13.0 | all-reduce | flops 960 | bytes 7680 | tf_op jit(solution)/shard_map/pmax | solution.py:18
  133.0 17.2 %psum.45 = f32[960]{0:T(1024)S(1)} all-reduce(f32[960]{0:T(1024)S(1)} %exponential_multiply_fusion), channel_id=1, replica_groups=mesh['src'=8,'tgt'=4] {'src'}, use_global_device_ids=true, to_apply=%region_15.0 | all-reduce | flops 960 | bytes 7680 | tf_op jit(solution)/shard_map/psum | solution.py:19
  150.2 1.4 fusion.13
  151.7 20.9 %reduce-scatter.2.cloned.1.call-done = f32[128,300]{0,1:T(8,128)} async-done(((f32[512,300]{0,1:T(8,128)}), f32[128,300]{0,1:T(8,128)}) %reduce-scatter.2.cloned.1.call-update) | async-done | bytes 153616 | tf_op jit(solution)/shard_map/reduce_scatter | solution.py:58
  172.5 2.0 convolution_bitcast_fusion
  174.8 33.7 %all-reduce.3.cloned.1.call-done = f32[300,300]{0,1:T(8,128)} async-done(((f32[300,300]{0,1:T(8,128)}), f32[300,300]{0,1:T(8,128)}) %all-reduce.3.cloned.1.call-update) | async-done | bytes 360016 | tf_op jit(solution)/shard_map/psum | solution.py:62
  209.6 74.9 %all-reduce.5.cloned.1.call-done = f32[300,300]{0,1:T(8,128)} async-done(((f32[300,300]{0,1:T(8,128)}), f32[300,300]{0,1:T(8,128)}) %all-reduce.5.cloned.1.call-update) | async-done | bytes 360016 | tf_op jit(solution)/shard_map/psum | solution.py:62
  284.5 1.8 multiply_reduce_fusion
  287.0 2.2 fusion.16
  289.3 1.2 fusion.11
  293.8 1.2 fusion.9
  298.3 1.2 fusion.7
  299.6 1.3 fusion.22
  307.6 1.2 fusion.3
  312.1 1.5 fusion.1
  314.6 1.2 fusion
  (48 shorter events, 25.0 us)
Async XLA Ops:
  7.2 34.2 %copy-start = (bf16[128,300]{0,1:T(8,128)(2,1)S(1)}, bf16[128,300]{0,1:T(8,128)(2,1)}, u32[]{:S(2)}) copy-start(bf16[128,300]{0,1:T(8,128)(2,1)} %param.2) | copy-start | bytes 230404
  7.2 165.4 %reduce-scatter.2.cloned.1.call-start = ((), (), s32[]{:S(2)}) async-start(), calls=%async_computation.1 | async-start | bytes 778240 | tf_op jit(solution)/shard_map/reduce_scatter | solution.py:58
  151.6 56.8 %all-reduce.3.cloned.1.call-start = ((), (), s32[]{:S(2)}) async-start(), calls=%async_computation.2 | async-start | bytes 933888 | tf_op jit(solution)/shard_map/psum | solution.py:62
  174.6 110.0 %all-reduce.5.cloned.1.call-start = ((), (), s32[]{:S(2)}) async-start(), calls=%async_computation.3 | async-start | bytes 933888 | tf_op jit(solution)/shard_map/psum | solution.py:62
  284.5 4.8 %copy-start.1 = (f32[300,300]{0,1:T(8,128)S(1)}, f32[300,300]{0,1:T(8,128)}, u32[]{:S(2)}) copy-start(f32[300,300]{0,1:T(8,128)} %all-reduce.5.cloned.1.call-done) | copy-start | bytes 1080004
Sparse Core Ops, SparseCore 0:
  151.7 20.7 reduce-scatter.1
  175.5 32.9 all-reduce.2
  211.9 72.6 all-reduce.4
